TPU v7x, 256 devices: a whole 4x4x8 slice. The times are simulated.
256 devices in a mesh: box: 32 (over y_hi, z, core), dir: 8 (over y_lo, x).
Axes of the slice: x: 4, y: 4 (y_hi: 2, y_lo: 2; y = y_hi * 2 + y_lo), z: 8, core: 2. Of those that a mesh axis runs over, the one named last changes fastest.
Arguments:
- leaf_density: bfloat16 [2048, 96, 8, 128], P('box', 'dir'), may hold values from -6 to 6
- phases_first: float32 [8, 96, 64], P(None, 'dir'), may hold values from -3.140625 to 3.140625
- phases_switch: float32 [8, 384, 64], P(None, 'dir'), may hold values from -3.140625 to 3.140625
- phases_top: float32 [8, 1536, 64], P(None, ('box', 'dir')), may hold values from -3.140625 to 3.140625
- transfer_first: bfloat16 [96, 2, 64, 512], P('dir'), may hold values from -0.1875 to 0.1875
- transfer_switch: bfloat16 [384, 2, 64, 512], P('dir'), may hold values from -0.1875 to 0.1875
- transfer_top: bfloat16 [1536, 2, 64, 512], P(('box', 'dir')), may hold values from -0.1875 to 0.1875
- child_mid: int32 [384], P('dir'), may hold values from 0 to 95, as said below
- child_top: int32 [1536], replicated, may hold values from 0 to 383, as said below
Outputs:
- top_density: float32 [4, 1536, 8, 128], P(None, ('box', 'dir'))
Inputs may be any that keep to these rules, and one draw needn't show every extreme that they name: `child_mid`: each level-1 wedge contains exactly 4 level-2 wedges. Each level-2 wedge contains exactly 4 level-3 wedges; with j = (w // 6) mod 8, child_top[w] lies in the level-2 wedges j * 48 to (j + 1) * 48 - 1.
All inputs are finite; a program needn't handle non-finite values.
Results may differ from a plain program's by a relative error of at most 0.0064.
Values may be sent and summed in bfloat16 or wider, within the bound.
No kernel may reach another device: no remote copies, remote signals or barrier semaphores. Data moves between devices by JAX's collectives and lax.ppermute only.
A program may use at most 64 MiB of HBM per device.

v0:
```python
import jax
import jax.numpy as jnp
from jax import lax
from jax.sharding import PartitionSpec as P


def lift_level(density, angles, transfer):
    box_count, wedges, excite, full_width = density.shape
    half_width = full_width // 2
    parents = box_count // 8
    children = density.reshape(parents, 8, wedges, excite, full_width).astype(jnp.float32)
    real_part = children[..., :half_width]
    imag_part = children[..., half_width:]
    cos_part = jnp.cos(angles)[None, :, :, None, :]
    sine_part = jnp.sin(angles)[None, :, :, None, :]
    phased = jnp.stack(
        [
            cos_part * real_part - sine_part * imag_part,
            sine_part * real_part + cos_part * imag_part,
        ],
        axis=4,
    ).astype(jnp.bfloat16)
    blocks = transfer.reshape(wedges, 2, half_width, 8, half_width)
    product = jnp.einsum("pcwnsr,wtkcr->pwnstk", phased, blocks, preferred_element_type=jnp.float32)
    real_out = product[..., 0, 0, :] - product[..., 1, 1, :]
    imag_out = product[..., 1, 0, :] + product[..., 0, 1, :]
    return jnp.concatenate([real_out, imag_out], axis=-1)


def shards(
    leaf_density,
    phases_first,
    phases_switch,
    phases_top,
    transfer_first,
    transfer_switch,
    transfer_top,
    child_mid,
    child_top,
):
    level_one = lift_level(leaf_density, phases_first, transfer_first).astype(jnp.bfloat16)
    all_low = lax.all_gather(level_one, "dir", axis=1, tiled=True)
    selected = jnp.take(all_low, child_mid, axis=1)
    level_two = lift_level(selected, phases_switch, transfer_switch).astype(jnp.bfloat16)
    mid_local = level_two.shape[1]
    top_count = transfer_top.shape[0]
    dir_index = lax.axis_index("dir")
    box_index = lax.axis_index("box")
    dir_count = lax.axis_size("dir")
    share_start = dir_index * mid_local
    every_box = lax.all_gather(level_two, "box", axis=0, tiled=True)
    own_start = (box_index * dir_count + dir_index) * top_count
    own_table = lax.dynamic_slice_in_dim(child_top, own_start, top_count, 0) - share_start
    top_input = jnp.take(every_box, own_table, axis=1)
    return lift_level(top_input, phases_top, transfer_top)


def solution(mesh):
    placed = (
        P("box", "dir", None, None),
        P(None, "dir", None),
        P(None, "dir", None),
        P(None, ("box", "dir"), None),
        P("dir", None, None, None),
        P("dir", None, None, None),
        P(("box", "dir"), None, None, None),
        P("dir"),
        P(),
    )
    return jax.shard_map(
        shards,
        mesh=mesh,
        in_specs=placed,
        out_specs=P(None, ("box", "dir"), None, None),
        check_vma=False,
    )
```

profile of v0, /device:TPU:1, one launch (start us, length us, event | category | flops | bytes accessed | tf_op | source)
XLA Modules:
  0.0 171.6 jit_solution(9915890975607049855)
XLA Ops:
  6.5 0.0 all-gather.3.cloned.1.call-start
  6.5 1.0 fusion.45
  7.5 1.7 copy.27
  9.2 5.2 %reshape.133 = bf16[12,2,64,8,64]{4,3,2,1,0:T(8,128)(2,1)} reshape(bf16[12,2,64,512]{3,2,1,0:T(8,128)(2,1)} %param.13) | data formatting | bytes 3145728 | tf_op jit(solution)/shard_map/reshape | solution.py:23
  14.4 0.0 copy-start
  14.4 1.2 fusion.6
  15.5 0.7 copy-done
  16.2 1.6 fusion.12
  17.9 0.0 copy-start.2
  17.9 0.1 fusion.31
  17.9 0.1 fusion.32
  18.0 0.8 pad_maximum_fusion
  18.8 0.0 all-gather.3.cloned.1.call-update
  18.9 0.0 all-gather.5.cloned.1.call-start
  18.9 0.0 copy-done.2
  18.9 0.7 fusion.44
  19.6 0.1 copy.26
  19.7 0.1 copy.32
  19.8 0.0 copy-start.4
  19.8 16.3 %reshape.134 = bf16[48,2,64,8,64]{4,3,2,1,0:T(8,128)(2,1)} reshape(bf16[48,2,64,512]{3,2,1,0:T(8,128)(2,1)} %param.14) | data formatting | bytes 12582912 | tf_op jit(solution)/shard_map/reshape | solution.py:23
  36.0 0.0 copy-done.4
  36.1 23.9 %all-gather.3.cloned.1.call-done = bf16[8,96,8,128]{3,2,0,1:T(8,128)(2,1)} async-done(((bf16[8,12,8,128]{3,2,0,1:T(8,128)(2,1)}), bf16[8,96,8,128]{3,2,0,1:T(8,128)(2,1)}) %all-gather.3.cloned.1.call-update) | async-done | bytes 1572880 | tf_op jit(solution)/shard_map/all_gather | solution.py:42
  60.0 2.1 %gather_fusion = bf16[48,8,8,128]{3,2,1,0:T(8,128)(2,1)S(1)} fusion(bf16[8,96,8,128]{3,2,0,1:T(8,128)(2,1)} %all-gather.3.cloned.1.call-done, s32[1024]{0:T(1024)S(1)} %pad_clamp_fusion.1), kind=kCustom, calls=%fused_computation | custom fusion | bytes 1573056 | tf_op jit(solution)/shard_map/jit(_take)/gather | solution.py:43
  62.1 0.2 fusion.25
  62.3 0.7 fusion.21
  63.0 7.9 %fusion.15 = f32[1,48,8,2,2,64]{5,2,4,3,1,0:T(8,128)S(1)} fusion(bf16[48,2,64,8,64,1]{4,3,2,1,0,5:T(8,128)(2,1)} %bitcast.126, bf16[8,48,8,1,64]{4,2,0,3,1:T(8,128)(2,1)S(1)} %get-tuple-element.10, bf16[8,48,8,1,64]{4,2,0,3,1:T(8,128)(2,1)S(1)} %get-tuple-element.9), kind=kOutput, calls=%fused_computation.21 | convolution fusion | flops 102236160 | bytes 7471104 | tf_op jit(solution)/shard_map/pcwnsr,wtkcr->pwnstk/dot_general | solution.py:24
  70.9 0.0 copy-start.1
  71.0 0.0 copy-start.3
  71.0 0.7 pad_maximum_fusion.1
  71.8 0.0 all-gather.5.cloned.1.call-update
  71.8 0.3 copy-done.1
  72.1 0.8 reshape.135
  72.9 0.8 compare_and_fusion.1
  73.7 0.0 copy-done.3
  73.7 0.1 fusion.46
  73.8 86.1 %all-gather.5.cloned.1.call-done = bf16[32,48,8,128]{3,2,1,0:T(8,128)(2,1)} async-done(((bf16[1,48,8,128]{3,2,1,0:T(8,128)(2,1)}), bf16[32,48,8,128]{3,2,1,0:T(8,128)(2,1)}) %all-gather.5.cloned.1.call-update) | async-done | bytes 3145744 | tf_op jit(solution)/shard_map/all_gather | solution.py:51
  160.0 2.6 %gather_fusion.1 = bf16[6,32,8,128]{3,2,1,0:T(8,128)(2,1)S(1)} fusion(bf16[32,48,8,128]{3,2,1,0:T(8,128)(2,1)} %all-gather.5.cloned.1.call-done, s32[1024]{0:T(1024)S(1)} %pad_clamp_fusion), kind=kCustom, calls=%fused_computation.1 | custom fusion | bytes 786456 | tf_op jit(solution)/shard_map/jit(_take)/gather | solution.py:54
  162.5 0.1 select_convert_fusion
  162.7 0.4 fusion.26
  163.1 0.9 fusion.18
  164.0 0.1 pad_maximum_fusion.2
  164.1 0.6 copy.41
  (8 shorter events, 0.1 us)
Async XLA Ops:
  6.5 53.5 %all-gather.3.cloned.1.call-start = ((), (), s32[]{:S(2)}) async-start(), calls=%async_computation | async-start | bytes 1769472 | tf_op jit(solution)/shard_map/all_gather | solution.py:42
  14.4 1.9 %copy-start = (bf16[12,2,64,8,64]{4,3,2,1,0:T(8,128)(2,1)S(1)}, bf16[12,2,64,8,64]{4,3,2,1,0:T(8,128)(2,1)}, u32[]{:S(2)}) copy-start(bf16[12,2,64,8,64]{4,3,2,1,0:T(8,128)(2,1)} %reshape.133) | copy-start | bytes 4718596
  17.9 1.0 copy-start.2
  18.9 141.1 %all-gather.5.cloned.1.call-start = ((), (), s32[]{:S(2)}) async-start(), calls=%async_computation.1 | async-start | bytes 3244032 | tf_op jit(solution)/shard_map/all_gather | solution.py:51
  19.8 16.3 %copy-start.4 = (s32[48]{0:T(128)S(1)}, s32[48]{0:T(128)}, u32[]{:S(2)}) copy-start(s32[48]{0:T(128)} %param.16) | copy-start | bytes 580
  70.9 1.2 copy-start.1
  71.0 2.7 %copy-start.3 = (f32[8,6,64]{2,0,1:T(8,128)S(1)}, f32[8,6,64]{2,0,1:T(8,128)}, u32[]{:S(2)}) copy-start(f32[8,6,64]{2,0,1:T(8,128)} %param.12) | copy-start | bytes 36868
Sparse Core Ops, SparseCore 0:
  19.0 40.9 all-gather.2
  71.9 88.0 all-gather.4
where the time goes:
time: 172 us
  waiting for transfers between devices  110 us (64%)
  local copies, waits for them, and re-layouts  32.2 us (19%)
  between operations  13.6 us (8%)
  matrix products  10.4 us (6%)
  other arithmetic  5.25 us (3%)
    all_gather x1, waiting for transfers between devices, shards(): every_box = lax.all_gather(level_two, 'box', axis=0, tiled=True)  86.1 us
    all_gather x1, waiting for transfers between devices, shards(): all_low = lax.all_gather(level_one, 'dir', axis=1, tiled=True)  23.9 us
    reshape x3, local copies, waits for them, and re-layouts, lift_level(): blocks = transfer.reshape(wedges, 2, half_width, 8, half_width)  22.2 us
    dot_general x3, matrix products, lift_level(): jnp.einsum('pcwnsr,wtkcr->pwnstk', phased, blocks, preferred_element_type...  10.4 us
  transfers between devices with their start and end apart: 2, of which 2 were waited for; matrix products, arithmetic and copies ran while one was open for 11% of the time, Pallas kernels for 0%

commit v1 on v0

--- a/solution.py
+++ b/solution.py
@@ -2,6 +2,13 @@
 import jax.numpy as jnp
 from jax import lax
 from jax.sharding import PartitionSpec as P
+
+
+def exchange_gather(block, axis, dim):
+    peers = lax.axis_size(axis)
+    blocks = jnp.stack([block for _ in range(peers)])
+    blocks = lax.all_to_all(blocks, axis, split_axis=0, concat_axis=0)
+    return jnp.concatenate(blocks, axis=dim)
 
 
 def lift_level(density, angles, transfer):
@@ -39,7 +46,7 @@
     child_top,
 ):
     level_one = lift_level(leaf_density, phases_first, transfer_first).astype(jnp.bfloat16)
-    all_low = lax.all_gather(level_one, "dir", axis=1, tiled=True)
+    all_low = exchange_gather(level_one, "dir", 1)
     selected = jnp.take(all_low, child_mid, axis=1)
     level_two = lift_level(selected, phases_switch, transfer_switch).astype(jnp.bfloat16)
     mid_local = level_two.shape[1]

time: 172 us -> 154 us (0.90)
  waiting for transfers between devices: 110 us -> 86.4 us
  starting transfers between devices: 0.04 us -> 6.01 us
    all_gather x1 -> x0, waiting for transfers between devices: 23.9 us -> none  [shards(): all_low = lax.all_gather(level_one, 'dir', axis=1, tiled=True)]
    all_to_all x0 -> x1, starting transfers between devices: none -> 5.97 us  [exchange_gather(): blocks = lax.all_to_all(blocks, axis, split_axis=0, concat_axis=0)]
    all_to_all x0 -> x1, waiting for transfers between devices: none -> 4.3 us  [exchange_gather(): blocks = lax.all_to_all(blocks, axis, split_axis=0, concat_axis=0)]
    all_gather x1, waiting for transfers between devices: 86.1 us -> 82.1 us  [shards(): every_box = lax.all_gather(level_two, 'box', axis=0, tiled=True)]
  transfers between devices with their start and end apart: 2 -> 2, of which waited for: 2 -> 2; matrix products, arithmetic and copies ran while one was open for 11% -> 12% of each run, Pallas kernels for 0% -> 0%
where the time goes in v1:
time: 154 us; the launch traced here: 153 us
  waiting for transfers between devices  86.4 us (56%)
  local copies, waits for them, and re-layouts  32.5 us (21%)
  between operations  13.6 us (9%)
  matrix products  10.4 us (7%)
  starting transfers between devices  6.01 us (4%)
  other arithmetic  4.55 us (3%)
    all_gather x1, waiting for transfers between devices, shards(): every_box = lax.all_gather(level_two, 'box', axis=0, tiled=True)  82.1 us
    reshape x3, local copies, waits for them, and re-layouts, lift_level(): blocks = transfer.reshape(wedges, 2, half_width, 8, half_width)  22.2 us
    dot_general x3, matrix products, lift_level(): jnp.einsum('pcwnsr,wtkcr->pwnstk', phased, blocks, preferred_element_type...  10.4 us
    all_to_all x1, starting transfers between devices, exchange_gather(): blocks = lax.all_to_all(blocks, axis, split_axis=0, concat_axis=0)  5.97 us
    all_to_all x1, waiting for transfers between devices, exchange_gather(): blocks = lax.all_to_all(blocks, axis, split_axis=0, concat_axis=0)  4.3 us
  transfers between devices with their start and end apart: 2, of which 2 were waited for; matrix products, arithmetic and copies ran while one was open for 12% of the time, Pallas kernels for 0%

profile of v1, /device:TPU:1, one launch (start us, length us, event | category | flops | bytes accessed | tf_op | source)
XLA Modules:
  0.0 153.5 jit_solution(2466601171001001099)
XLA Ops:
  6.5 1.0 fusion.45
  7.5 1.7 %copy.45 = f32[64,12,8,128]{3,2,0,1:T(8,128)S(1)} copy(bf16[64,12,8,128]{3,2,1,0:T(8,128)(2,1)} %param.9) | data formatting | bytes 4718592 | tf_op jit(solution)/shard_map/convert_element_type | solution.py:18
  9.2 5.2 %reshape.146 = bf16[12,2,64,8,64]{4,3,2,1,0:T(8,128)(2,1)} reshape(bf16[12,2,64,512]{3,2,1,0:T(8,128)(2,1)} %param.13) | data formatting | bytes 3145728 | tf_op jit(solution)/shard_map/reshape | solution.py:30
  14.4 0.0 copy-start
  14.4 1.2 fusion.6
  15.6 0.7 copy-done
  16.3 1.6 %fusion.12 = f32[8,12,8,2,2,64]{5,2,4,3,0,1:T(8,128)S(1)} fusion(bf16[12,2,64,8,64,1,1]{4,3,2,1,0,6,5:T(8,128)(2,1)S(1)} %bitcast.131, bf16[8,8,12,8,1,64]{5,3,1,4,0,2:T(8,128)(2,1)S(1)} %get-tuple-element.8, bf16[8,8,12,8,1,64]{5,3,1,4,0,2:T(8,128)(2,1)S(1)} %get-tuple-element.7), kind=kOutput, calls=%fused_computation.20 | convolution fusion | flops 204472320 | bytes 3932160 | tf_op jit(solution)/shard_map/pcwnsr,wtkcr->pwnstk/dot_general | solution.py:31
  17.9 0.1 fusion.31
  17.9 0.1 fusion.32
  18.0 0.1 pad_maximum_fusion
  18.2 1.4 stack.47
  19.6 0.0 copy-start.2
  19.6 6.0 %all-to-all-start = ((bf16[8,8,12,8,128]{4,3,2,1,0:T(8,128)(2,1)}), bf16[8,8,12,8,128]{4,3,2,1,0:T(8,128)(2,1)S(1)}, u32[]{:S(2)}, u32[]{:S(2)}) async-start(bf16[8,8,12,8,128]{4,3,2,1,0:T(8,128)(2,1)} %stack.47), calls=%async_computation | async-start | bytes 3145728 | tf_op jit(solution)/shard_map/all_to_all | solution.py:10
  25.6 0.0 all-gather.2.cloned.1.call-start
  25.7 0.0 copy-done.2
  25.7 0.7 fusion.44
  26.4 0.1 copy.44
  26.4 0.1 copy.52
  26.5 0.0 copy-start.4
  26.5 16.3 %reshape.149 = bf16[48,2,64,8,64]{4,3,2,1,0:T(8,128)(2,1)} reshape(bf16[48,2,64,512]{3,2,1,0:T(8,128)(2,1)} %param.14) | data formatting | bytes 12582912 | tf_op jit(solution)/shard_map/reshape | solution.py:30
  42.8 0.0 copy-done.4
  42.8 4.3 %all-to-all-done = bf16[8,8,12,8,128]{4,3,2,1,0:T(8,128)(2,1)S(1)} async-done(((bf16[8,8,12,8,128]{4,3,2,1,0:T(8,128)(2,1)}), bf16[8,8,12,8,128]{4,3,2,1,0:T(8,128)(2,1)S(1)}, u32[]{:S(2)}, u32[]{:S(2)}) %all-to-all-start) | async-done | bytes 1572896 | tf_op jit(solution)/shard_map/all_to_all | solution.py:10
  47.1 0.1 copy.51
  47.2 0.8 gather_fusion
  48.1 0.2 fusion.25
  48.3 0.7 fusion.21
  49.0 7.9 %fusion.15 = f32[1,48,8,2,2,64]{5,2,4,3,1,0:T(8,128)S(1)} fusion(bf16[48,2,64,8,64,1]{4,3,2,1,0,5:T(8,128)(2,1)} %bitcast.129, bf16[8,48,8,1,64]{4,2,0,3,1:T(8,128)(2,1)S(1)} %get-tuple-element.10, bf16[8,48,8,1,64]{4,2,0,3,1:T(8,128)(2,1)S(1)} %get-tuple-element.9), kind=kOutput, calls=%fused_computation.21 | convolution fusion | flops 102236160 | bytes 7471104 | tf_op jit(solution)/shard_map/pcwnsr,wtkcr->pwnstk/dot_general | solution.py:31
  56.9 0.0 copy-start.1
  56.9 0.0 copy-start.3
  57.0 0.7 pad_maximum_fusion.1
  57.7 0.0 all-gather.2.cloned.1.call-update
  57.8 0.3 copy-done.1
  58.1 0.8 reshape.150
  58.9 0.8 compare_and_fusion.1
  59.7 0.0 copy-done.3
  59.7 0.1 fusion.46
  59.8 82.1 %all-gather.2.cloned.1.call-done = bf16[32,48,8,128]{3,2,1,0:T(8,128)(2,1)} async-done(((bf16[1,48,8,128]{3,2,1,0:T(8,128)(2,1)}), bf16[32,48,8,128]{3,2,1,0:T(8,128)(2,1)}) %all-gather.2.cloned.1.call-update) | async-done | bytes 3145744 | tf_op jit(solution)/shard_map/all_gather | solution.py:58
  141.9 2.6 %gather_fusion.1 = bf16[6,32,8,128]{3,2,1,0:T(8,128)(2,1)S(1)} fusion(bf16[32,48,8,128]{3,2,1,0:T(8,128)(2,1)} %all-gather.2.cloned.1.call-done, s32[1024]{0:T(1024)S(1)} %pad_clamp_fusion), kind=kCustom, calls=%fused_computation.1 | custom fusion | bytes 786456 | tf_op jit(solution)/shard_map/jit(_take)/gather | solution.py:61
  144.5 0.1 select_convert_fusion
  144.6 0.4 fusion.26
  145.0 0.9 fusion.18
  145.9 0.1 pad_maximum_fusion.2
  146.0 0.6 copy.61
  (9 shorter events, 0.2 us)
Async XLA Ops:
  14.4 1.9 %copy-start = (bf16[12,2,64,8,64]{4,3,2,1,0:T(8,128)(2,1)S(1)}, bf16[12,2,64,8,64]{4,3,2,1,0:T(8,128)(2,1)}, u32[]{:S(2)}) copy-start(bf16[12,2,64,8,64]{4,3,2,1,0:T(8,128)(2,1)} %reshape.146) | copy-start | bytes 4718596
  19.6 6.0 %copy-start.2 = (f32[8,48,64]{2,1,0:T(8,128)S(1)}, f32[8,48,64]{2,1,0:T(8,128)}, u32[]{:S(2)}) copy-start(f32[8,48,64]{2,1,0:T(8,128)} %param.11) | copy-start | bytes 294916
  19.6 27.5 %all-to-all-start = ((bf16[8,8,12,8,128]{4,3,2,1,0:T(8,128)(2,1)}), bf16[8,8,12,8,128]{4,3,2,1,0:T(8,128)(2,1)S(1)}, u32[]{:S(2)}, u32[]{:S(2)}) async-start(bf16[8,8,12,8,128]{4,3,2,1,0:T(8,128)(2,1)} %stack.47), calls=%async_computation | async-start | bytes 3145728 | tf_op jit(solution)/shard_map/all_to_all | solution.py:10
  25.6 116.3 %all-gather.2.cloned.1.call-start = ((), (), s32[]{:S(2)}) async-start(), calls=%async_computation.1 | async-start | bytes 3244032 | tf_op jit(solution)/shard_map/all_gather | solution.py:58
  26.5 16.3 %copy-start.4 = (s32[48]{0:T(128)S(1)}, s32[48]{0:T(128)}, u32[]{:S(2)}) copy-start(s32[48]{0:T(128)} %param.16) | copy-start | bytes 580
  56.9 1.2 copy-start.1
  56.9 2.7 %copy-start.3 = (f32[8,6,64]{2,0,1:T(8,128)S(1)}, f32[8,6,64]{2,0,1:T(8,128)}, u32[]{:S(2)}) copy-start(f32[8,6,64]{2,0,1:T(8,128)} %param.12) | copy-start | bytes 36868
Sparse Core Ops, SparseCore 0:
  57.9 83.9 all-gather.1
